TPU v7x, 32 devices: a whole 2x2x4 slice. The times are simulated.
32 devices in a mesh: ctx: 2 (over core), shard: 16 (over z, y, x).
Axes of the slice: x: 2, y: 2, z: 4, core: 2. Of those that a mesh axis runs over, the one named last changes fastest.
Arguments:
- tokens: bfloat16 [2, 16, 1024, 768], P(None, 'shard', 'ctx'), may hold values from -6 to 6
- cotangent: bfloat16 [2, 16, 1024, 768], P(None, 'shard', 'ctx'), may hold values from -6 to 6
- segment_ids: int32 [2, 16, 1024], P(None, 'shard', 'ctx'), may hold values from 0 to 1, never falling along the last dimension, each value on 1 to 896 neighbouring positions
- padding: int32 [2, 16, 1024], P(None, 'shard', 'ctx'), may hold values 0 or 1
- routes: int32 [2, 16, 1024, 1], P(None, 'shard', 'ctx'), may hold values from 0 to 15; in each aligned block of 512 rows (0 to 511, 512 to 1023, ..., all dimensions but the last counted through in order) at most 64 rows name the same one
- norm_one_gain: bfloat16 [768], replicated, may hold values from 0.5 to 1.5
- qkv_weight: bfloat16 [768, 2304], P('shard'), may hold values from -0.21875 to 0.21875
- out_weight: bfloat16 [768, 768], P('shard'), may hold values from -1.75 to 1.75
- norm_two_gain: bfloat16 [768], replicated, may hold values from 0.5 to 1.5
- centroids: bfloat16 [768, 16], replicated, may hold values from -0.15625 to 0.15625
- expert_in: bfloat16 [16, 768, 3072], P('shard'), may hold values from -0.21875 to 0.21875
- expert_out: bfloat16 [16, 3072, 768], P('shard'), may hold values from -0.21875 to 0.21875
Outputs:
- block_out: bfloat16 [2, 16, 1024, 768], P(None, 'shard', 'ctx')
- grad_tokens: float32 [2, 16, 1024, 768], P(None, 'shard', 'ctx')
- grad_norm_one: float32 [768], P(('ctx', 'shard'))
- grad_qkv: float32 [768, 2304], P(('ctx', 'shard'))
- grad_out_proj: float32 [768, 768], P(('ctx', 'shard'))
- grad_norm_two: float32 [768], P(('ctx', 'shard'))
- grad_centroids: float32 [768, 16], P(('ctx', 'shard'))
- grad_expert_in: float32 [16, 768, 3072], P('shard', None, 'ctx')
- grad_expert_out: float32 [16, 3072, 768], P('shard', 'ctx')
Inputs may be any that keep to these rules, and one draw needn't show every extreme that they name: `segment_ids`: segment ids never fall along a sequence; each sequence holds two documents, each of at least 128 and at most 896 positions; where the split falls varies from sequence to sequence. `routes`: within each aligned block of 512 positions of a sequence, no expert is named more than 64 times; some block names some expert exactly 64 times.
All inputs are finite; a program needn't handle non-finite values. No bound on the sum of `padding` on one device may be relied on, other than what follows from the above.
Results may differ from a plain program's by a relative error of at most 0.013.
Values may be sent and summed in bfloat16 or wider, within the bound.
A program may use at most 384 MiB of HBM per device.

v0:
```python
import jax
import jax.numpy as jnp
from jax import lax
from jax.sharding import PartitionSpec as P

D = 768
HEADS = 12
HEAD_DIM = 64
FF = 3072
MICRO = 2
EPSILON = 1e-05
NEGATIVE = -1e30
HIGH = lax.Precision.HIGHEST


def layer_norm(values, gain_vec):
    centre = values - jnp.mean(values, axis=1, keepdims=True)
    spread = jnp.mean(centre * centre, axis=1, keepdims=True)
    return centre * lax.rsqrt(spread + EPSILON) * gain_vec


def gelu_tanh(values):
    return jax.nn.gelu(values, approximate=True)


def masked_scores(queries, key_heads, query_pos, key_pos, query_doc, key_doc, key_pad):
    scores = jnp.einsum(
        "qhd,khd->hqk", queries, key_heads, preferred_element_type=jnp.float32
    ) * HEAD_DIM ** (-0.5)
    allowed = (query_doc[:, None] == key_doc[None, :]) & (key_pos[None, :] <= query_pos[:, None])
    allowed = allowed & ((key_pad[None, :] == 1) | (key_pos[None, :] == query_pos[:, None]))
    return jnp.where(allowed[None], scores, NEGATIVE)


def rows_first(left, right):
    return lax.dot_general(
        left, right, (((0,), (0,)), ((), ())), preferred_element_type=jnp.float32
    )


def rows_last(left, right):
    return lax.dot_general(
        left, right, (((1,), (1,)), ((), ())), preferred_element_type=jnp.float32
    )


def body(
    tokens,
    cotangent,
    segment_ids,
    padding,
    routes,
    norm_one_gain,
    qkv_weight,
    out_weight,
    norm_two_gain,
    centroids,
    expert_in,
    expert_out,
):
    local_len = tokens.shape[2]
    experts = centroids.shape[1]
    capacity = max(2, 2 * local_len // experts)
    seq_len = local_len * lax.axis_size("ctx")
    qkv_full, out_full = (
        lax.all_gather(qkv_weight, "shard", axis=0, tiled=True),
        lax.all_gather(out_weight, "shard", axis=0, tiled=True),
    )
    gain_one = norm_one_gain.astype(jnp.float32)
    gain_two = norm_two_gain.astype(jnp.float32)
    centre_f = centroids.astype(jnp.float32)
    up_local = expert_in[0]
    down_local = expert_out[0]
    query_pos = lax.axis_index("ctx") * local_len + jnp.arange(local_len, dtype=jnp.int32)
    all_pos = jnp.arange(seq_len, dtype=jnp.int32)
    slot_ids = jnp.arange(experts * capacity, dtype=jnp.int32)
    expert_ids = jnp.arange(experts, dtype=jnp.int32)
    score_scale = HEAD_DIM ** (-0.5)
    grad_qkv_sum = jnp.zeros((D, 3 * D), jnp.float32)
    grad_out_sum = jnp.zeros((D, D), jnp.float32)
    grad_one_sum = jnp.zeros((D,), jnp.float32)
    grad_two_sum = jnp.zeros((D,), jnp.float32)
    grad_centre = jnp.zeros((D, experts), jnp.float32)
    grad_up_sum = jnp.zeros((D, FF), jnp.float32)
    grad_down_sum = jnp.zeros((D, FF), jnp.float32)
    block_list = []
    input_list = []
    for micro_index in range(MICRO):
        inputs = tokens[micro_index, 0].astype(jnp.float32)
        doc_ids = segment_ids[micro_index, 0]
        pad_mask = padding[micro_index, 0]
        route_ids = routes[micro_index, 0, :, 0]
        normed_one, norm_one_back = jax.vjp(layer_norm, inputs, gain_one)
        first_bf = normed_one.astype(jnp.bfloat16)
        qkv = jnp.dot(first_bf, qkv_full, preferred_element_type=jnp.float32)
        queries = qkv[:, :D].astype(jnp.bfloat16)
        key_rows = qkv[:, D : 2 * D].astype(jnp.bfloat16)
        value_rows = qkv[:, 2 * D :].astype(jnp.bfloat16)
        key_all, value_all, doc_all, pad_all = (
            lax.all_gather(key_rows, "ctx", axis=0, tiled=True),
            lax.all_gather(value_rows, "ctx", axis=0, tiled=True),
            lax.all_gather(doc_ids, "ctx", axis=0, tiled=True),
            lax.all_gather(pad_mask, "ctx", axis=0, tiled=True),
        )
        query_heads = queries.reshape(local_len, HEADS, HEAD_DIM)
        key_heads = key_all.reshape(seq_len, HEADS, HEAD_DIM)
        value_heads = value_all.reshape(seq_len, HEADS, HEAD_DIM)
        scores = masked_scores(
            query_heads, key_heads, query_pos, all_pos, doc_ids, doc_all, pad_all
        )
        row_max = jnp.max(scores, axis=2, keepdims=True)
        weights = jnp.exp(scores - row_max)
        row_total = jnp.sum(weights, axis=2, keepdims=True)
        probs_now = weights / row_total
        log_total = row_max + jnp.log(row_total)
        attended = jnp.einsum(
            "hqk,khd->qhd",
            probs_now.astype(jnp.bfloat16),
            value_heads,
            preferred_element_type=jnp.float32,
        )
        attended = attended.reshape(local_len, D).astype(jnp.bfloat16)
        residual = inputs + jnp.dot(attended, out_full, preferred_element_type=jnp.float32)
        normed_two, norm_two_back = jax.vjp(layer_norm, residual, gain_two)
        second_bf = normed_two.astype(jnp.bfloat16)
        choose_mask = route_ids[:, None] == expert_ids[None, :]
        choose_f = choose_mask.astype(jnp.float32)
        logit = jnp.sum(
            jnp.dot(second_bf, centroids, preferred_element_type=jnp.float32) * choose_f, axis=1
        )
        gate_value = jax.nn.sigmoid(logit)
        choose_int = choose_mask.astype(jnp.int32)
        counts = jnp.cumsum(choose_int, axis=0)
        slot_rank = jnp.sum(counts * choose_int, axis=1) - 1
        target = route_ids * capacity + slot_rank
        dispatch = (slot_ids[:, None] == target[None, :]).astype(jnp.bfloat16)
        outbound = jnp.dot(dispatch, second_bf, preferred_element_type=jnp.float32).astype(
            jnp.bfloat16
        )
        outbound = outbound.reshape(experts, capacity, D)
        received = lax.all_to_all(outbound, "shard", split_axis=0, concat_axis=0, tiled=True)
        slot_rows = received.reshape(-1, D)
        upward = jnp.dot(slot_rows, up_local, preferred_element_type=jnp.float32)
        hidden = gelu_tanh(upward).astype(jnp.bfloat16)
        result = jnp.dot(hidden, down_local, preferred_element_type=jnp.float32).astype(
            jnp.bfloat16
        )
        returned = lax.all_to_all(
            result.reshape(received.shape), "shard", split_axis=0, concat_axis=0, tiled=True
        )
        returned, received, upward = (
            returned,
            received,
            upward.reshape(received.shape[0], received.shape[1], FF),
        )
        expert_rows = rows_first(dispatch, returned.reshape(experts * capacity, D))
        block_list.append((residual + gate_value[:, None] * expert_rows).astype(jnp.bfloat16))
        grad_out = cotangent[micro_index, 0].astype(jnp.float32)
        grad_gate = jnp.sum(grad_out * expert_rows, axis=1)
        grad_logit = grad_gate * gate_value * (1.0 - gate_value)
        grad_rows = (gate_value[:, None] * grad_out).astype(jnp.bfloat16)
        grad_outbound = jnp.dot(dispatch, grad_rows, preferred_element_type=jnp.float32).astype(
            jnp.bfloat16
        )
        grad_received = lax.all_to_all(
            grad_outbound.reshape(experts, capacity, D),
            "shard",
            split_axis=0,
            concat_axis=0,
            tiled=True,
        )
        grad_result = grad_received.reshape(-1, D)
        hidden_again, gelu_back = jax.vjp(gelu_tanh, upward.reshape(-1, FF))
        grad_down_sum = grad_down_sum + rows_first(grad_result, hidden_again.astype(jnp.bfloat16))
        grad_hidden = rows_last(grad_result, down_local)
        grad_upward = gelu_back(grad_hidden)[0].astype(jnp.bfloat16)
        grad_up_sum = grad_up_sum + rows_first(received.reshape(-1, D), grad_upward)
        grad_send = (
            rows_last(grad_upward, up_local).astype(jnp.bfloat16).reshape(grad_received.shape)
        )
        grad_back = lax.all_to_all(grad_send, "shard", split_axis=0, concat_axis=0, tiled=True)
        grad_second = rows_first(dispatch, grad_back.reshape(experts * capacity, D))
        grad_second = grad_second + grad_logit[:, None] * jnp.dot(
            choose_f, centre_f.T, precision=HIGH
        )
        grad_centre = grad_centre + jnp.dot(
            second_bf.astype(jnp.float32).T, choose_f * grad_logit[:, None], precision=HIGH
        )
        grad_resid_norm, grad_two_term = norm_two_back(grad_second)
        grad_residual = grad_out + grad_resid_norm
        grad_two_sum = grad_two_sum + grad_two_term
        grad_branch = grad_residual.astype(jnp.bfloat16)
        grad_out_sum = grad_out_sum + rows_first(attended, grad_branch)
        grad_attend = (
            rows_last(grad_branch, out_full)
            .astype(jnp.bfloat16)
            .reshape(local_len, HEADS, HEAD_DIM)
        )
        probs_again = jnp.exp(
            masked_scores(query_heads, key_heads, query_pos, all_pos, doc_ids, doc_all, pad_all)
            - log_total
        )
        grad_probs = jnp.einsum(
            "qhd,khd->hqk", grad_attend, value_heads, preferred_element_type=jnp.float32
        )
        row_terms = jnp.sum(probs_again * grad_probs, axis=2, keepdims=True)
        grad_scores = (probs_again * (grad_probs - row_terms)).astype(jnp.bfloat16)
        grad_query = (
            jnp.einsum("hqk,khd->qhd", grad_scores, key_heads, preferred_element_type=jnp.float32)
            * score_scale
        )
        grad_key_all = (
            jnp.einsum("hqk,qhd->khd", grad_scores, query_heads, preferred_element_type=jnp.float32)
            * score_scale
        )
        grad_value_all = jnp.einsum(
            "hqk,qhd->khd",
            probs_again.astype(jnp.bfloat16),
            grad_attend,
            preferred_element_type=jnp.float32,
        )
        grad_key, grad_value = (
            lax.psum_scatter(
                grad_key_all.reshape(seq_len, D).astype(jnp.bfloat16),
                "ctx",
                scatter_dimension=0,
                tiled=True,
            ).astype(jnp.float32),
            lax.psum_scatter(
                grad_value_all.reshape(seq_len, D).astype(jnp.bfloat16),
                "ctx",
                scatter_dimension=0,
                tiled=True,
            ).astype(jnp.float32),
        )
        grad_qkv_rows = jnp.concatenate(
            [grad_query.reshape(local_len, D), grad_key, grad_value], axis=1
        ).astype(jnp.bfloat16)
        grad_qkv_sum = grad_qkv_sum + rows_first(first_bf, grad_qkv_rows)
        grad_first = rows_last(grad_qkv_rows, qkv_full)
        grad_in_norm, grad_one_term = norm_one_back(grad_first)
        grad_one_sum = grad_one_sum + grad_one_term
        input_list.append(grad_residual + grad_in_norm)
    dense_sums = (
        lax.psum_scatter(grad_one_sum, ("ctx", "shard"), scatter_dimension=0, tiled=True),
        lax.psum_scatter(grad_qkv_sum, ("ctx", "shard"), scatter_dimension=0, tiled=True),
        lax.psum_scatter(grad_out_sum, ("ctx", "shard"), scatter_dimension=0, tiled=True),
        lax.psum_scatter(grad_two_sum, ("ctx", "shard"), scatter_dimension=0, tiled=True),
        lax.psum_scatter(grad_centre, ("ctx", "shard"), scatter_dimension=0, tiled=True),
    )
    expert_sums = (
        lax.psum_scatter(
            grad_up_sum.astype(jnp.bfloat16), "ctx", scatter_dimension=1, tiled=True
        ).astype(jnp.float32),
        lax.psum_scatter(
            grad_down_sum.astype(jnp.bfloat16), "ctx", scatter_dimension=1, tiled=True
        ).astype(jnp.float32),
    )
    block_out = jnp.stack(block_list)[:, None]
    grad_tokens = jnp.stack(input_list)[:, None]
    return (
        block_out,
        grad_tokens,
        dense_sums[0],
        dense_sums[1],
        dense_sums[2],
        dense_sums[3],
        dense_sums[4],
        expert_sums[0][None],
        expert_sums[1].T[None],
    )


def solution(mesh):
    in_specs = (
        P(None, "shard", "ctx", None),
        P(None, "shard", "ctx", None),
        P(None, "shard", "ctx"),
        P(None, "shard", "ctx"),
        P(None, "shard", "ctx", None),
        P(),
        P("shard", None),
        P("shard", None),
        P(),
        P(),
        P("shard", None, None),
        P("shard", None, None),
    )
    out_specs = (
        P(None, "shard", "ctx", None),
        P(None, "shard", "ctx", None),
        P(("ctx", "shard")),
        P(("ctx", "shard"), None),
        P(("ctx", "shard"), None),
        P(("ctx", "shard")),
        P(("ctx", "shard"), None),
        P("shard", None, "ctx"),
        P("shard", "ctx", None),
    )
    return jax.shard_map(body, mesh=mesh, in_specs=in_specs, out_specs=out_specs, check_vma=False)
```

profile of v0, /device:TPU:0, one launch (start us, length us, event | category | flops | bytes accessed | tf_op | source)
XLA Modules:
  0.0 985.1 jit_solution(11996730696689875057)
XLA Ops:
  11.0 73.8 %all-gather.11.cloned.1.call-done = bf16[768,2304]{1,0:T(8,128)(2,1)} async-done(((bf16[48,2304]{1,0:T(8,128)(2,1)}), bf16[768,2304]{1,0:T(8,128)(2,1)}) %all-gather.11.cloned.1.call-update) | async-done | bytes 3538960 | tf_op jit(solution)/shard_map/all_gather | solution.py:66
  113.1 12.7 %fusion.27 = (f32[12,512]{1,0:T(8,128)S(1)}, f32[12,512,1024]{2,1,0:T(8,128)}) fusion(pred[512,1024]{1,0:T(8,128)(4,1)} %get-tuple-element.91, bf16[512,12,64]{0,2,1:T(8,128)(2,1)} %bitcast.293, bf16[1024,12,64]{0,2,1:T(8,128)(2,1)S(1)} %bitcast.289), kind=kOutput, calls=%fused_computation.45 | convolution fusion | flops 824174592 | bytes 28073984 | tf_op jit(solution)/shard_map/qhd,khd->hqk/dot_general | solution.py:27
  125.8 11.8 %fusion.1 = f32[12,512]{1,0:T(8,128)S(1)} fusion(f32[12,512]{1,0:T(8,128)S(1)} %get-tuple-element.96, f32[12,512,1024]{2,1,0:T(8,128)} %get-tuple-element.97, pred[512,1024]{1,0:T(8,128)(4,1)S(1)} %copy-done.14), kind=kLoop, calls=%fused_computation.13 | loop fusion | flops 25159680 | bytes 25739264 | tf_op jit(solution)/shard_map/reduce_sum | solution.py:113
  140.3 12.6 %fusion.112 = bf16[12,64,512]{2,1,0:T(8,128)(2,1)} fusion(bf16[1024,12,64]{0,2,1:T(8,128)(2,1)} %bitcast.299, f32[12,512]{1,0:T(8,128)S(1)} %fusion.1, f32[12,512]{1,0:T(8,128)S(1)} %get-tuple-element.96, f32[12,512,1024]{2,1,0:T(8,128)} %get-tuple-element.97, pred[512,1024]{1,0:T(8,128)(4,1)S(1)} %copy-done.15), kind=kOutput, calls=%fused_computation.162 | convolution fusion | flops 837156864 | bytes 28098560 | tf_op jit(solution)/shard_map/hqk,khd->qhd/dot_general | solution.py:116
  153.0 18.9 %all-gather.17.cloned.1.call-done = bf16[768,768]{1,0:T(8,128)(2,1)} async-done(((bf16[48,768]{1,0:T(8,128)(2,1)}), bf16[768,768]{1,0:T(8,128)(2,1)}) %all-gather.17.cloned.1.call-update) | async-done | bytes 1179664 | tf_op jit(solution)/shard_map/all_gather | solution.py:67
  185.3 15.0 %fusion.26 = (f32[12,512]{1,0:T(8,128)S(1)}, f32[12,512,1024]{2,1,0:T(8,128)}) fusion(pred[512,1024]{1,0:T(8,128)(4,1)} %get-tuple-element.90, bf16[512,12,64]{0,2,1:T(8,128)(2,1)} %bitcast.295, bf16[1024,12,64]{0,2,1:T(8,128)(2,1)} %bitcast.291), kind=kOutput, calls=%fused_computation.44 | convolution fusion | flops 824174592 | bytes 28073984 | tf_op jit(solution)/shard_map/qhd,khd->hqk/dot_general | solution.py:27
  200.4 11.8 %fusion = f32[12,512]{1,0:T(8,128)S(1)} fusion(f32[12,512]{1,0:T(8,128)S(1)} %get-tuple-element.92, f32[12,512,1024]{2,1,0:T(8,128)} %get-tuple-element.93, pred[512,1024]{1,0:T(8,128)(4,1)S(1)} %copy-done.17), kind=kLoop, calls=%fused_computation.12 | loop fusion | flops 25159680 | bytes 25739264 | tf_op jit(solution)/shard_map/reduce_sum | solution.py:113
  214.7 11.9 %fusion.113 = bf16[12,64,512]{2,1,0:T(8,128)(2,1)S(1)} fusion(bf16[1024,12,64]{0,2,1:T(8,128)(2,1)} %bitcast.301, f32[12,512]{1,0:T(8,128)S(1)} %fusion, f32[12,512]{1,0:T(8,128)S(1)} %get-tuple-element.92, f32[12,512,1024]{2,1,0:T(8,128)} %get-tuple-element.93, pred[512,1024]{1,0:T(8,128)(4,1)} %get-tuple-element.90), kind=kOutput, calls=%fused_computation.163 | convolution fusion | flops 837156864 | bytes 28098560 | tf_op jit(solution)/shard_map/hqk,khd->qhd/dot_general | solution.py:116
  241.5 30.6 %all-to-all-done.2 = bf16[16,64,768]{2,1,0:T(8,128)(2,1)} async-done(((bf16[16,64,768]{2,1,0:T(8,128)(2,1)}), bf16[16,64,768]{2,1,0:T(8,128)(2,1)}, u32[]{:S(2)}, u32[]{:S(2)}) %all-to-all-start.2) | async-done | bytes 1572896 | tf_op jit(solution)/shard_map/all_to_all | solution.py:141
  303.0 11.2 %all-to-all-done = bf16[16,64,768]{2,1,0:T(8,128)(2,1)} async-done(((bf16[16,64,768]{2,1,0:T(8,128)(2,1)}), bf16[16,64,768]{2,1,0:T(8,128)(2,1)}, u32[]{:S(2)}, u32[]{:S(2)}) %all-to-all-start) | async-done | bytes 1572896 | tf_op jit(solution)/shard_map/all_to_all | solution.py:141
  344.2 11.0 %all-to-all-done.3 = bf16[16,64,768]{2,1,0:T(8,128)(2,1)} async-done(((bf16[16,64,768]{2,1,0:T(8,128)(2,1)}), bf16[16,64,768]{2,1,0:T(8,128)(2,1)}, u32[]{:S(2)}, u32[]{:S(2)}) %all-to-all-start.3) | async-done | bytes 1572896 | tf_op jit(solution)/shard_map/all_to_all | solution.py:148
  367.0 29.4 %all-to-all-done.1 = bf16[16,64,768]{2,1,0:T(8,128)(2,1)} async-done(((bf16[16,64,768]{2,1,0:T(8,128)(2,1)}), bf16[16,64,768]{2,1,0:T(8,128)(2,1)}, u32[]{:S(2)}, u32[]{:S(2)}) %all-to-all-start.1) | async-done | bytes 1572896 | tf_op jit(solution)/shard_map/all_to_all | solution.py:148
  414.8 29.7 %all-to-all-done.6 = bf16[16,64,768]{2,1,0:T(8,128)(2,1)} async-done(((bf16[16,64,768]{2,1,0:T(8,128)(2,1)}), bf16[16,64,768]{2,1,0:T(8,128)(2,1)}, u32[]{:S(2)}, u32[]{:S(2)}) %all-to-all-start.6) | async-done | bytes 1572896 | tf_op jit(solution)/shard_map/all_to_all | solution.py:165
  452.2 15.4 %fusion.17 = bf16[1024,3072]{1,0:T(8,128)(2,1)S(1)} fusion(f32[1024,3072]{1,0:T(8,128)} %copy-done.93, bf16[1024,768]{1,0:T(8,128)(2,1)} %bitcast.53, bf16[1,3072,768]{2,1,0:T(8,128)(2,1)} %param.23), kind=kOutput, calls=%fused_computation.33 | convolution fusion | flops 4894752768 | bytes 25165824 | tf_op jit(solution)/shard_map/dot_general | solution.py:42
  493.2 14.2 %fusion.10 = bf16[1024,3072]{1,0:T(8,128)(2,1)S(1)} fusion(f32[1024,3072]{1,0:T(8,128)} %copy-done.94, bf16[1024,768]{1,0:T(8,128)(2,1)S(1)} %bitcast.309, bf16[1,3072,768]{2,1,0:T(8,128)(2,1)} %param.23), kind=kOutput, calls=%fused_computation.26 | convolution fusion | flops 4894752768 | bytes 25165824 | tf_op jit(solution)/shard_map/dot_general | solution.py:42
  540.2 27.5 %all-to-all-done.5 = bf16[16,64,768]{2,1,0:T(8,128)(2,1)} async-done(((bf16[16,64,768]{2,1,0:T(8,128)(2,1)}), bf16[16,64,768]{2,1,0:T(8,128)(2,1)}, u32[]{:S(2)}, u32[]{:S(2)}) %all-to-all-start.5) | async-done | bytes 1572896 | tf_op jit(solution)/shard_map/all_to_all | solution.py:181
  582.2 17.9 %multiply_reduce_fusion.1 = (f32[12,512]{1,0:T(8,128)S(1)}, f32[12,512,1024]{2,1,0:T(8,128)}) fusion(f32[12,512]{1,0:T(8,128)S(1)} %log_add_fusion.1, f32[12,512,1024]{2,1,0:T(8,128)} %get-tuple-element.93, pred[512,1024]{1,0:T(8,128)(4,1)S(1)} %copy-done.18, bf16[512,12,64]{0,2,1:T(8,128)(2,1)} %bitcast.307, bf16[1024,12,64]{0,2,1:T(8,128)(2,1)S(1)} %bitcast.302), kind=kOutput, calls=%fused_computation.4 | convolution fusion | flops 836757504 | bytes 53264384 | tf_op jit(solution)/shard_map/qhd,khd->hqk/dot_general | solution.py:203
  600.1 16.9 %multiply_convert_fusion.1 = bf16[12,512,1024]{2,1,0:T(8,128)(2,1)S(1)} fusion(f32[12,512,1024]{2,1,0:T(8,128)} %get-tuple-element.103, f32[12,512]{1,0:T(8,128)S(1)} %get-tuple-element.102, f32[12,512]{1,0:T(8,128)S(1)} %log_add_fusion.1, f32[12,512,1024]{2,1,0:T(8,128)} %get-tuple-element.93, pred[512,1024]{1,0:T(8,128)(4,1)S(1)} %copy-done.18), kind=kLoop, calls=%fused_computation.3 | loop fusion | flops 37748736 | bytes 63488000 | tf_op jit(solution)/shard_map/convert_element_type | solution.py:207
  625.4 13.9 %fusion.94 = bf16[12,64,1024]{2,1,0:T(8,128)(2,1)} fusion(bf16[512,12,64]{0,2,1:T(8,128)(2,1)S(1)} %bitcast.308, f32[12,512]{1,0:T(8,128)S(1)} %log_add_fusion.1, f32[12,512,1024]{2,1,0:T(8,128)} %get-tuple-element.93, pred[512,1024]{1,0:T(8,128)(4,1)S(1)} %copy-done.18), kind=kOutput, calls=%fused_computation.129 | convolution fusion | flops 831258624 | bytes 28073984 | tf_op jit(solution)/shard_map/hqk,qhd->khd/dot_general | solution.py:216
  640.8 17.9 %multiply_reduce_fusion = (f32[12,512]{1,0:T(8,128)S(1)}, f32[12,512,1024]{2,1,0:T(8,128)}) fusion(f32[12,512]{1,0:T(8,128)S(1)} %log_add_fusion, f32[12,512,1024]{2,1,0:T(8,128)} %get-tuple-element.97, pred[512,1024]{1,0:T(8,128)(4,1)S(1)} %copy-done.16, bf16[512,12,64]{0,2,1:T(8,128)(2,1)} %bitcast.305, bf16[1024,12,64]{0,2,1:T(8,128)(2,1)S(1)} %bitcast.300), kind=kOutput, calls=%fused_computation.1 | convolution fusion | flops 836757504 | bytes 53264384 | tf_op jit(solution)/shard_map/qhd,khd->hqk/dot_general | solution.py:203
  658.6 16.9 %multiply_convert_fusion = bf16[12,512,1024]{2,1,0:T(8,128)(2,1)S(1)} fusion(f32[12,512,1024]{2,1,0:T(8,128)} %get-tuple-element.105, f32[12,512]{1,0:T(8,128)S(1)} %get-tuple-element.104, f32[12,512]{1,0:T(8,128)S(1)} %log_add_fusion, f32[12,512,1024]{2,1,0:T(8,128)} %get-tuple-element.97, pred[512,1024]{1,0:T(8,128)(4,1)S(1)} %copy-done.16), kind=kLoop, calls=%fused_computation | loop fusion | flops 37748736 | bytes 63488000 | tf_op jit(solution)/shard_map/convert_element_type | solution.py:207
  680.6 13.1 %fusion.97 = bf16[12,64,1024]{2,1,0:T(8,128)(2,1)} fusion(bf16[512,12,64]{0,2,1:T(8,128)(2,1)S(1)} %bitcast.306, f32[12,512]{1,0:T(8,128)S(1)} %log_add_fusion, f32[12,512,1024]{2,1,0:T(8,128)} %get-tuple-element.97, pred[512,1024]{1,0:T(8,128)(4,1)S(1)} %copy-done.16), kind=kOutput, calls=%fused_computation.130 | convolution fusion | flops 831258624 | bytes 28073984 | tf_op jit(solution)/shard_map/hqk,qhd->khd/dot_general | solution.py:216
  786.4 45.6 %all-reduce.3 = (f32[768]{0:T(1024)S(1)}, f32[768]{0:T(1024)S(1)}, f32[768,16]{0,1:T(8,128)S(1)}) all-reduce(f32[768]{0:T(1024)S(1)} %add.227, f32[768]{0:T(1024)S(1)} %add.230, f32[768,16]{0,1:T(8,128)S(1)} %convolution_add_fusion.2), channel_id=10, replica_groups=mesh['ctx'=2,'shard'=16] {'ctx','shard'}, use_global_device_ids=true, to_apply=%region_38.39.clone | all-reduce | flops 13824 | bytes 110592
  854.4 123.8 %reduce-scatter.18.cloned.1.call-done = f32[24,2304]{1,0:T(8,128)} async-done(((f32[768,2304]{1,0:T(8,128)}), f32[24,2304]{1,0:T(8,128)}) %reduce-scatter.18.cloned.1.call-update) | async-done | bytes 221200 | tf_op jit(solution)/shard_map/reduce_scatter | solution.py:246
  (354 shorter events, 365.9 us)
Async XLA Ops:
  7.2 355.7 %copy-start = (bf16[768,16]{0,1:T(8,128)(2,1)S(1)}, bf16[768,16]{0,1:T(8,128)(2,1)}, u32[]{:S(2)}) copy-start(bf16[768,16]{0,1:T(8,128)(2,1)} %param.21) | copy-start | bytes 73732
  7.2 77.6 %all-gather.11.cloned.1.call-start = ((), (), s32[]{:S(2)}) async-start(), calls=%async_computation.16 | async-start | bytes 3760128 | tf_op jit(solution)/shard_map/all_gather | solution.py:66
  7.9 103.4 %all-gather.21.cloned.1.call-start = ((), (), s32[]{:S(2)}) async-start(), calls=%async_computation.21 | async-start | bytes 2359296 | tf_op jit(solution)/shard_map/all_gather | solution.py:100
  90.3 47.4 %all-gather.19.cloned.1.call-start = ((), (), s32[]{:S(2)}) async-start(), calls=%async_computation.20 | async-start | bytes 2359296 | tf_op jit(solution)/shard_map/all_gather | solution.py:101
  91.0 80.9 %all-gather.17.cloned.1.call-start = ((), (), s32[]{:S(2)}) async-start(), calls=%async_computation.19 | async-start | bytes 1253376 | tf_op jit(solution)/shard_map/all_gather | solution.py:67
  91.6 91.0 %all-gather.15.cloned.1.call-start = ((), (), s32[]{:S(2)}) async-start(), calls=%async_computation.18 | async-start | bytes 2359296 | tf_op jit(solution)/shard_map/all_gather | solution.py:100
  91.7 443.0 %copy-start.57 = (s32[1,1,512,1]{2,3,1,0:T(1,128)}, s32[1,1,512,1]{2,3,1,0:T(1,128)S(1)}, u32[]{:S(2)}) copy-start(s32[1,1,512,1]{2,3,1,0:T(1,128)S(1)} %get-tuple-element.78) | copy-start | bytes 6148
  98.4 113.7 %all-gather.13.cloned.1.call-start = ((), (), s32[]{:S(2)}) async-start(), calls=%async_computation.17 | async-start | bytes 2359296 | tf_op jit(solution)/shard_map/all_gather | solution.py:101
  230.9 41.2 %all-to-all-start.2 = ((bf16[16,64,768]{2,1,0:T(8,128)(2,1)}), bf16[16,64,768]{2,1,0:T(8,128)(2,1)}, u32[]{:S(2)}, u32[]{:S(2)}) async-start(bf16[16,64,768]{2,1,0:T(8,128)(2,1)} %bitcast.313), calls=%async_computation.2 | async-start | bytes 3145728 | tf_op jit(solution)/shard_map/all_to_all | solution.py:141
  272.1 42.1 %all-to-all-start = ((bf16[16,64,768]{2,1,0:T(8,128)(2,1)}), bf16[16,64,768]{2,1,0:T(8,128)(2,1)}, u32[]{:S(2)}, u32[]{:S(2)}) async-start(bf16[16,64,768]{2,1,0:T(8,128)(2,1)} %bitcast.316), calls=%async_computation | async-start | bytes 3145728 | tf_op jit(solution)/shard_map/all_to_all | solution.py:141
  314.3 41.0 %all-to-all-start.3 = ((bf16[16,64,768]{2,1,0:T(8,128)(2,1)}), bf16[16,64,768]{2,1,0:T(8,128)(2,1)}, u32[]{:S(2)}, u32[]{:S(2)}) async-start(bf16[16,64,768]{2,1,0:T(8,128)(2,1)} %bitcast.317), calls=%async_computation.3 | async-start | bytes 3145728 | tf_op jit(solution)/shard_map/all_to_all | solution.py:148
  355.3 41.1 %all-to-all-start.1 = ((bf16[16,64,768]{2,1,0:T(8,128)(2,1)}), bf16[16,64,768]{2,1,0:T(8,128)(2,1)}, u32[]{:S(2)}, u32[]{:S(2)}) async-start(bf16[16,64,768]{2,1,0:T(8,128)(2,1)} %bitcast.315), calls=%async_computation.1 | async-start | bytes 3145728 | tf_op jit(solution)/shard_map/all_to_all | solution.py:148
  403.5 40.9 %all-to-all-start.6 = ((bf16[16,64,768]{2,1,0:T(8,128)(2,1)}), bf16[16,64,768]{2,1,0:T(8,128)(2,1)}, u32[]{:S(2)}, u32[]{:S(2)}) async-start(bf16[16,64,768]{2,1,0:T(8,128)(2,1)} %bitcast.318), calls=%async_computation.8 | async-start | bytes 3145728 | tf_op jit(solution)/shard_map/all_to_all | solution.py:165
  444.5 41.2 %all-to-all-start.4 = ((bf16[16,64,768]{2,1,0:T(8,128)(2,1)}), bf16[16,64,768]{2,1,0:T(8,128)(2,1)S(1)}, u32[]{:S(2)}, u32[]{:S(2)}) async-start(bf16[16,64,768]{2,1,0:T(8,128)(2,1)} %bitcast.319), calls=%async_computation.4 | async-start | bytes 3145728 | tf_op jit(solution)/shard_map/all_to_all | solution.py:165
  485.7 41.1 %all-to-all-start.7 = ((bf16[16,64,768]{2,1,0:T(8,128)(2,1)}), bf16[16,64,768]{2,1,0:T(8,128)(2,1)}, u32[]{:S(2)}, u32[]{:S(2)}) async-start(bf16[16,64,768]{2,1,0:T(8,128)(2,1)} %bitcast.320), calls=%async_computation.9 | async-start | bytes 3145728 | tf_op jit(solution)/shard_map/all_to_all | solution.py:181
  526.8 40.9 %all-to-all-start.5 = ((bf16[16,64,768]{2,1,0:T(8,128)(2,1)}), bf16[16,64,768]{2,1,0:T(8,128)(2,1)}, u32[]{:S(2)}, u32[]{:S(2)}) async-start(bf16[16,64,768]{2,1,0:T(8,128)(2,1)} %bitcast.314), calls=%async_computation.5 | async-start | bytes 3145728 | tf_op jit(solution)/shard_map/all_to_all | solution.py:181
  534.2 222.7 %reduce-scatter.10.cloned.1.call-start = ((), (), s32[]{:S(2)}) async-start(), calls=%async_computation.22 | async-start | bytes 2359296 | tf_op jit(solution)/shard_map/reduce_scatter | solution.py:223
  622.0 135.0 %reduce-scatter.12.cloned.1.call-start = ((), (), s32[]{:S(2)}) async-start(), calls=%async_computation.23 | async-start | bytes 2359296 | tf_op jit(solution)/shard_map/reduce_scatter | solution.py:229
  639.4 124.5 %reduce-scatter.14.cloned.1.call-start = ((), (), s32[]{:S(2)}) async-start(), calls=%async_computation.24 | async-start | bytes 2359296 | tf_op jit(solution)/shard_map/reduce_scatter | solution.py:223
  680.5 83.3 %reduce-scatter.16.cloned.1.call-start = ((), (), s32[]{:S(2)}) async-start(), calls=%async_computation.25 | async-start | bytes 2359296 | tf_op jit(solution)/shard_map/reduce_scatter | solution.py:229
  693.7 145.6 %reduce-scatter.24.cloned.1.call-start = ((), (), s32[]{:S(2)}) async-start(), calls=%async_computation.29 | async-start | bytes 7077888 | tf_op jit(solution)/shard_map/reduce_scatter | solution.py:255
  713.6 136.3 %reduce-scatter.22.cloned.1.call-start = ((), (), s32[]{:S(2)}) async-start(), calls=%async_computation.28 | async-start | bytes 7077888 | tf_op jit(solution)/shard_map/reduce_scatter | solution.py:252
  731.4 123.0 %reduce-scatter.20.cloned.1.call-start = ((), (), s32[]{:S(2)}) async-start(), calls=%async_computation.27 | async-start | bytes 2433024 | tf_op jit(solution)/shard_map/reduce_scatter | solution.py:247
  735.8 242.4 %reduce-scatter.18.cloned.1.call-start = ((), (), s32[]{:S(2)}) async-start(), calls=%async_computation.26 | async-start | bytes 7299072 | tf_op jit(solution)/shard_map/reduce_scatter | solution.py:246
  (93 other events, 1828.0 us)
Sparse Core Ops, SparseCore 0:
  10.8 73.9 all-gather.10
  90.4 8.3 all-gather.20
  100.9 10.9 all-gather.18
  114.6 57.2 all-gather.16
  173.9 8.6 all-gather.14
  184.6 10.9 all-gather.12
  622.1 10.7 reduce-scatter.9
  639.5 10.7 reduce-scatter.11
  680.7 11.1 reduce-scatter.13
  694.6 11.0 reduce-scatter.15
  713.7 15.1 reduce-scatter.23
  731.7 14.8 reduce-scatter.21
  752.5 100.3 reduce-scatter.19
  859.9 118.1 reduce-scatter.17
where the time goes:
time: 992 us; the launch traced here: 985 us
  waiting for transfers between devices  381 us (38%)
  matrix products  336 us (34%)
  other arithmetic  88.3 us (9%)
  starting transfers between devices  60.9 us (6%)
  blocking collectives  53.2 us (5%)
  local copies, waits for them, and re-layouts  49.9 us (5%)
  between operations  15.8 us (2%)
    reduce_scatter x1, waiting for transfers between devices, body(): lax.psum_scatter(grad_qkv_sum, ('ctx', 'shard'), scatter_dimension=0, til...  124 us
    dot_general x12, matrix products, rows_first(): lax.dot_general(left, right, (((0,), (0,)), ((), ())), preferred_element_...  73.9 us
    all_gather x1, waiting for transfers between devices, body(): lax.all_gather(qkv_weight, 'shard', axis=0, tiled=True)  73.8 us
    dot_general x8, matrix products, rows_last(): lax.dot_general(left, right, (((1,), (1,)), ((), ())), preferred_element_...  57.5 us
    unnamed x1, blocking collectives  45.6 us
    all_to_all x2, waiting for transfers between devices, body(): lax.all_to_all(outbound, 'shard', split_axis=0, concat_axis=0, tiled=True)  41.8 us
    all_to_all x2, waiting for transfers between devices, body(): lax.all_to_all(result.reshape(received.shape), 'shard', split_axis=0, con...  40.4 us
    all_to_all x2, waiting for transfers between devices, body(): lax.all_to_all(grad_outbound.reshape(experts, capacity, D), 'shard', spli...  36.7 us
  transfers between devices with their start and end apart: 22, of which 12 were waited for; matrix products, arithmetic and copies ran while one was open for 37% of the time, Pallas kernels for 0%

commit v1 on v0

--- a/solution.py
+++ b/solution.py
@@ -11,6 +11,17 @@
 EPSILON = 1e-05
 NEGATIVE = -1e30
 HIGH = lax.Precision.HIGHEST
+
+
+def in_blocks(value, dim, peers):
+    before, after = (value.shape[:dim], value.shape[dim + 1 :])
+    return jnp.moveaxis(value.reshape(*before, peers, -1, *after), dim, 0)
+
+
+def in_order(parts, dim):
+    lengths = list(parts.shape[1:])
+    lengths[dim] *= parts.shape[0]
+    return jnp.moveaxis(parts, 0, dim).reshape(lengths)
 
 
 def layer_norm(values, gain_vec):
@@ -145,9 +156,15 @@
         result = jnp.dot(hidden, down_local, preferred_element_type=jnp.float32).astype(
             jnp.bfloat16
         )
-        returned = lax.all_to_all(
-            result.reshape(received.shape), "shard", split_axis=0, concat_axis=0, tiled=True
-        )
+        array = result.reshape(received.shape)
+        count, index = (lax.axis_size("shard"), lax.axis_index("shard"))
+        blocks = in_blocks(array, 0, count)
+        gathered = [blocks[index]]
+        for lap in range(1, count):
+            sent = blocks[index ^ lap]
+            gathered.append(lax.ppermute(sent, "shard", [(i, i ^ lap) for i in range(count)]))
+        blocks = jnp.stack(gathered)[index ^ jnp.arange(count)]
+        returned = in_order(blocks, 0)
         returned, received, upward = (
             returned,
             received,

time: 992 us -> 1030 us (1.038)
  starting transfers between devices: 60.9 us -> 105 us
  waiting for transfers between devices: 381 us -> 341 us
  local copies, waits for them, and re-layouts: 49.9 us -> 77.3 us
    ppermute x0 -> x30, starting transfers between devices: none -> 57.1 us  [body(): lax.ppermute(sent, 'shard', [(i, i ^ lap) for i in range(count)])]
    all_to_all x2 -> x0, waiting for transfers between devices: 40.4 us -> none  [body(): lax.all_to_all(result.reshape(received.shape), 'shard', split_axis=0, con...]
    unnamed x194 -> x244, local copies, waits for them, and re-layouts: 31.4 us -> 48.8 us
    all_to_all x2 -> x0, starting transfers between devices: 14.9 us -> none  [body(): lax.all_to_all(result.reshape(received.shape), 'shard', split_axis=0, con...]
  transfers between devices with their start and end apart: 22 -> 50, of which waited for: 12 -> 13; matrix products, arithmetic and copies ran while one was open for 37% -> 39% of each run, Pallas kernels for 0% -> 0%
where the time goes in v1:
time: 1030 us; the launch traced here: 1020 us
  waiting for transfers between devices  341 us (33%)
  matrix products  340 us (33%)
  starting transfers between devices  105 us (10%)
  other arithmetic  87 us (8%)
  local copies, waits for them, and re-layouts  77.3 us (8%)
  blocking collectives  51.8 us (5%)
  between operations  16 us (2%)
    reduce_scatter x1, waiting for transfers between devices, body(): lax.psum_scatter(grad_qkv_sum, ('ctx', 'shard'), scatter_dimension=0, til...  123 us
    all_gather x1, waiting for transfers between devices, body(): lax.all_gather(qkv_weight, 'shard', axis=0, tiled=True)  73.8 us
    dot_general x12, matrix products, rows_first(): lax.dot_general(left, right, (((0,), (0,)), ((), ())), preferred_element_...  70.7 us
    dot_general x8, matrix products, rows_last(): lax.dot_general(left, right, (((1,), (1,)), ((), ())), preferred_element_...  57.5 us
    ppermute x30, starting transfers between devices, body(): lax.ppermute(sent, 'shard', [(i, i ^ lap) for i in range(count)])  57.1 us
    unnamed x244, local copies, waits for them, and re-layouts  48.8 us
    unnamed x1, blocking collectives  44.5 us
    all_to_all x2, waiting for transfers between devices, body(): lax.all_to_all(grad_send, 'shard', split_axis=0, concat_axis=0, tiled=True)  35.8 us
  transfers between devices with their start and end apart: 50, of which 13 were waited for; matrix products, arithmetic and copies ran while one was open for 39% of the time, Pallas kernels for 0%

profile of v1, /device:TPU:0, one launch (start us, length us, event | category | flops | bytes accessed | tf_op | source)
XLA Modules:
  0.0 1018.4 jit_solution(12546534493265613377)
XLA Ops:
  11.0 73.8 %all-gather.11.cloned.1.call-done = bf16[768,2304]{1,0:T(8,128)(2,1)} async-done(((bf16[48,2304]{1,0:T(8,128)(2,1)}), bf16[768,2304]{1,0:T(8,128)(2,1)}) %all-gather.11.cloned.1.call-update) | async-done | bytes 3538960 | tf_op jit(solution)/shard_map/all_gather | solution.py:77
  112.8 12.8 %fusion.27 = (f32[12,512]{1,0:T(8,128)S(1)}, f32[12,512,1024]{2,1,0:T(8,128)}) fusion(pred[512,1024]{1,0:T(8,128)(4,1)} %get-tuple-element.123, bf16[512,12,64]{0,2,1:T(8,128)(2,1)} %bitcast.417, bf16[1024,12,64]{0,2,1:T(8,128)(2,1)S(1)} %bitcast.413), kind=kOutput, calls=%fused_computation.47 | convolution fusion | flops 824174592 | bytes 28073984 | tf_op jit(solution)/shard_map/qhd,khd->hqk/dot_general | solution.py:38
  125.6 11.8 %fusion.1 = f32[12,512]{1,0:T(8,128)S(1)} fusion(f32[12,512]{1,0:T(8,128)S(1)} %get-tuple-element.128, f32[12,512,1024]{2,1,0:T(8,128)} %get-tuple-element.129, pred[512,1024]{1,0:T(8,128)(4,1)S(1)} %copy-done.14), kind=kLoop, calls=%fused_computation.15 | loop fusion | flops 25159680 | bytes 25739264 | tf_op jit(solution)/shard_map/reduce_sum | solution.py:124
  140.1 12.7 %fusion.112 = bf16[12,64,512]{2,1,0:T(8,128)(2,1)} fusion(bf16[1024,12,64]{0,2,1:T(8,128)(2,1)} %bitcast.423, f32[12,512]{1,0:T(8,128)S(1)} %fusion.1, f32[12,512]{1,0:T(8,128)S(1)} %get-tuple-element.128, f32[12,512,1024]{2,1,0:T(8,128)} %get-tuple-element.129, pred[512,1024]{1,0:T(8,128)(4,1)S(1)} %copy-done.15), kind=kOutput, calls=%fused_computation.164 | convolution fusion | flops 837156864 | bytes 28098560 | tf_op jit(solution)/shard_map/hqk,khd->qhd/dot_general | solution.py:127
  152.8 19.1 %all-gather.17.cloned.1.call-done = bf16[768,768]{1,0:T(8,128)(2,1)} async-done(((bf16[48,768]{1,0:T(8,128)(2,1)}), bf16[768,768]{1,0:T(8,128)(2,1)}) %all-gather.17.cloned.1.call-update) | async-done | bytes 1179664 | tf_op jit(solution)/shard_map/all_gather | solution.py:78
  185.6 15.0 %fusion.26 = (f32[12,512]{1,0:T(8,128)S(1)}, f32[12,512,1024]{2,1,0:T(8,128)}) fusion(pred[512,1024]{1,0:T(8,128)(4,1)} %get-tuple-element.122, bf16[512,12,64]{0,2,1:T(8,128)(2,1)} %bitcast.419, bf16[1024,12,64]{0,2,1:T(8,128)(2,1)} %bitcast.415), kind=kOutput, calls=%fused_computation.46 | convolution fusion | flops 824174592 | bytes 28073984 | tf_op jit(solution)/shard_map/qhd,khd->hqk/dot_general | solution.py:38
  200.5 11.8 %fusion = f32[12,512]{1,0:T(8,128)S(1)} fusion(f32[12,512]{1,0:T(8,128)S(1)} %get-tuple-element.124, f32[12,512,1024]{2,1,0:T(8,128)} %get-tuple-element.125, pred[512,1024]{1,0:T(8,128)(4,1)S(1)} %copy-done.17), kind=kLoop, calls=%fused_computation.14 | loop fusion | flops 25159680 | bytes 25739264 | tf_op jit(solution)/shard_map/reduce_sum | solution.py:124
  214.9 11.9 %fusion.113 = bf16[12,64,512]{2,1,0:T(8,128)(2,1)S(1)} fusion(bf16[1024,12,64]{0,2,1:T(8,128)(2,1)} %bitcast.425, f32[12,512]{1,0:T(8,128)S(1)} %fusion, f32[12,512]{1,0:T(8,128)S(1)} %get-tuple-element.124, f32[12,512,1024]{2,1,0:T(8,128)} %get-tuple-element.125, pred[512,1024]{1,0:T(8,128)(4,1)} %get-tuple-element.122), kind=kOutput, calls=%fused_computation.165 | convolution fusion | flops 837156864 | bytes 28098560 | tf_op jit(solution)/shard_map/hqk,khd->qhd/dot_general | solution.py:127
  242.5 30.0 %all-to-all-done = bf16[16,64,768]{2,1,0:T(8,128)(2,1)} async-done(((bf16[16,64,768]{2,1,0:T(8,128)(2,1)}), bf16[16,64,768]{2,1,0:T(8,128)(2,1)}, u32[]{:S(2)}, u32[]{:S(2)}) %all-to-all-start) | async-done | bytes 1572896 | tf_op jit(solution)/shard_map/all_to_all | solution.py:152
  288.1 13.4 %fusion.88 = bf16[1024,768]{1,0:T(8,128)(2,1)S(1)} fusion(bf16[1,3072,768]{2,1,0:T(8,128)(2,1)} %param.23, f32[1024,3072]{1,0:T(8,128)S(1)} %fusion.42), kind=kOutput, calls=%fused_computation.129 | convolution fusion | flops 4860936192 | bytes 18874368 | tf_op jit(solution)/shard_map/dot_general | solution.py:156
  321.9 13.6 %fusion.91 = bf16[1024,768]{1,0:T(8,128)(2,1)S(1)} fusion(bf16[1,3072,768]{2,1,0:T(8,128)(2,1)} %param.23, f32[1024,3072]{1,0:T(8,128)S(1)} %fusion.40), kind=kOutput, calls=%fused_computation.130 | convolution fusion | flops 4860936192 | bytes 18874368 | tf_op jit(solution)/shard_map/dot_general | solution.py:156
  447.0 28.0 %all-to-all-done.4 = bf16[16,64,768]{2,1,0:T(8,128)(2,1)} async-done(((bf16[16,64,768]{2,1,0:T(8,128)(2,1)}), bf16[16,64,768]{2,1,0:T(8,128)(2,1)}, u32[]{:S(2)}, u32[]{:S(2)}) %all-to-all-start.4) | async-done | bytes 1572896 | tf_op jit(solution)/shard_map/all_to_all | solution.py:182
  482.8 15.4 %fusion.17 = bf16[1024,3072]{1,0:T(8,128)(2,1)S(1)} fusion(f32[1024,3072]{1,0:T(8,128)} %copy-done.105, bf16[1024,768]{1,0:T(8,128)(2,1)} %bitcast.116, bf16[1,3072,768]{2,1,0:T(8,128)(2,1)} %param.23), kind=kOutput, calls=%fused_computation.35 | convolution fusion | flops 4894752768 | bytes 25165824 | tf_op jit(solution)/shard_map/dot_general | solution.py:53
  524.0 14.2 %fusion.10 = bf16[1024,3072]{1,0:T(8,128)(2,1)S(1)} fusion(f32[1024,3072]{1,0:T(8,128)} %copy-done.104, bf16[1024,768]{1,0:T(8,128)(2,1)S(1)} %bitcast.433, bf16[1,3072,768]{2,1,0:T(8,128)(2,1)} %param.23), kind=kOutput, calls=%fused_computation.28 | convolution fusion | flops 4894752768 | bytes 25165824 | tf_op jit(solution)/shard_map/dot_general | solution.py:53
  571.0 27.5 %all-to-all-done.3 = bf16[16,64,768]{2,1,0:T(8,128)(2,1)} async-done(((bf16[16,64,768]{2,1,0:T(8,128)(2,1)}), bf16[16,64,768]{2,1,0:T(8,128)(2,1)}, u32[]{:S(2)}, u32[]{:S(2)}) %all-to-all-start.3) | async-done | bytes 1572896 | tf_op jit(solution)/shard_map/all_to_all | solution.py:198
  613.1 17.9 %multiply_reduce_fusion.1 = (f32[12,512]{1,0:T(8,128)S(1)}, f32[12,512,1024]{2,1,0:T(8,128)}) fusion(f32[12,512]{1,0:T(8,128)S(1)} %log_add_fusion.1, f32[12,512,1024]{2,1,0:T(8,128)} %get-tuple-element.125, pred[512,1024]{1,0:T(8,128)(4,1)S(1)} %copy-done.18, bf16[512,12,64]{0,2,1:T(8,128)(2,1)} %bitcast.431, bf16[1024,12,64]{0,2,1:T(8,128)(2,1)S(1)} %bitcast.426), kind=kOutput, calls=%fused_computation.6 | convolution fusion | flops 836757504 | bytes 53264384 | tf_op jit(solution)/shard_map/qhd,khd->hqk/dot_general | solution.py:220
  631.0 16.9 %multiply_convert_fusion.1 = bf16[12,512,1024]{2,1,0:T(8,128)(2,1)S(1)} fusion(f32[12,512,1024]{2,1,0:T(8,128)} %get-tuple-element.135, f32[12,512]{1,0:T(8,128)S(1)} %get-tuple-element.134, f32[12,512]{1,0:T(8,128)S(1)} %log_add_fusion.1, f32[12,512,1024]{2,1,0:T(8,128)} %get-tuple-element.125, pred[512,1024]{1,0:T(8,128)(4,1)S(1)} %copy-done.18), kind=kLoop, calls=%fused_computation.5 | loop fusion | flops 37748736 | bytes 63488000 | tf_op jit(solution)/shard_map/convert_element_type | solution.py:224
  657.0 14.3 %fusion.94 = bf16[12,64,1024]{2,1,0:T(8,128)(2,1)} fusion(bf16[512,12,64]{0,2,1:T(8,128)(2,1)} %bitcast.432, f32[12,512]{1,0:T(8,128)S(1)} %log_add_fusion.1, f32[12,512,1024]{2,1,0:T(8,128)} %get-tuple-element.125, pred[512,1024]{1,0:T(8,128)(4,1)S(1)} %copy-done.18), kind=kOutput, calls=%fused_computation.131 | convolution fusion | flops 831258624 | bytes 28073984 | tf_op jit(solution)/shard_map/hqk,qhd->khd/dot_general | solution.py:233
  672.3 17.8 %multiply_reduce_fusion = (f32[12,512]{1,0:T(8,128)S(1)}, f32[12,512,1024]{2,1,0:T(8,128)}) fusion(f32[12,512]{1,0:T(8,128)S(1)} %log_add_fusion, f32[12,512,1024]{2,1,0:T(8,128)} %get-tuple-element.129, pred[512,1024]{1,0:T(8,128)(4,1)S(1)} %copy-done.16, bf16[512,12,64]{0,2,1:T(8,128)(2,1)} %bitcast.429, bf16[1024,12,64]{0,2,1:T(8,128)(2,1)S(1)} %bitcast.424), kind=kOutput, calls=%fused_computation.3 | convolution fusion | flops 836757504 | bytes 53264384 | tf_op jit(solution)/shard_map/qhd,khd->hqk/dot_general | solution.py:220
  690.1 16.9 %multiply_convert_fusion = bf16[12,512,1024]{2,1,0:T(8,128)(2,1)S(1)} fusion(f32[12,512,1024]{2,1,0:T(8,128)} %get-tuple-element.137, f32[12,512]{1,0:T(8,128)S(1)} %get-tuple-element.136, f32[12,512]{1,0:T(8,128)S(1)} %log_add_fusion, f32[12,512,1024]{2,1,0:T(8,128)} %get-tuple-element.129, pred[512,1024]{1,0:T(8,128)(4,1)S(1)} %copy-done.16), kind=kLoop, calls=%fused_computation.2 | loop fusion | flops 37748736 | bytes 63488000 | tf_op jit(solution)/shard_map/convert_element_type | solution.py:224
  713.1 13.4 %fusion.97 = bf16[12,64,1024]{2,1,0:T(8,128)(2,1)} fusion(bf16[512,12,64]{0,2,1:T(8,128)(2,1)S(1)} %bitcast.430, f32[12,512]{1,0:T(8,128)S(1)} %log_add_fusion, f32[12,512,1024]{2,1,0:T(8,128)} %get-tuple-element.129, pred[512,1024]{1,0:T(8,128)(4,1)S(1)} %copy-done.16), kind=kOutput, calls=%fused_computation.132 | convolution fusion | flops 831258624 | bytes 28073984 | tf_op jit(solution)/shard_map/hqk,qhd->khd/dot_general | solution.py:233
  771.3 11.0 %multiply_convert_fusion.7 = bf16[12,64,512]{2,1,0:T(8,128)(2,1)} fusion(bf16[1024,12,64]{0,2,1:T(8,128)(2,1)S(1)} %bitcast.416, bf16[12,512,1024]{2,1,0:T(8,128)(2,1)} %copy-done.2), kind=kOutput, calls=%fused_computation.153 | convolution fusion | flops 806092800 | bytes 14942208 | tf_op jit(solution)/shard_map/hqk,khd->qhd/dot_general | solution.py:226
  821.3 44.5 %all-reduce.3 = (f32[768]{0:T(1024)S(1)}, f32[768]{0:T(1024)S(1)}, f32[768,16]{0,1:T(8,128)S(1)}) all-reduce(f32[768]{0:T(1024)S(1)} %add.319, f32[768]{0:T(1024)S(1)} %add.322, f32[768,16]{0,1:T(8,128)S(1)} %convolution_add_fusion.2), channel_id=10, replica_groups=mesh['ctx'=2,'shard'=16] {'ctx','shard'}, use_global_device_ids=true, to_apply=%region_38.39.clone | all-reduce | flops 13824 | bytes 110592
  888.2 123.3 %reduce-scatter.18.cloned.1.call-done = f32[24,2304]{1,0:T(8,128)} async-done(((f32[768,2304]{1,0:T(8,128)}), f32[24,2304]{1,0:T(8,128)}) %reduce-scatter.18.cloned.1.call-update) | async-done | bytes 221200 | tf_op jit(solution)/shard_map/reduce_scatter | solution.py:263
  (468 shorter events, 415.7 us)
Async XLA Ops:
  7.2 77.6 %all-gather.11.cloned.1.call-start = ((), (), s32[]{:S(2)}) async-start(), calls=%async_computation.14 | async-start | bytes 3760128 | tf_op jit(solution)/shard_map/all_gather | solution.py:77
  7.9 103.2 %all-gather.21.cloned.1.call-start = ((), (), s32[]{:S(2)}) async-start(), calls=%async_computation.19 | async-start | bytes 2359296 | tf_op jit(solution)/shard_map/all_gather | solution.py:111
  90.3 47.2 %all-gather.19.cloned.1.call-start = ((), (), s32[]{:S(2)}) async-start(), calls=%async_computation.18 | async-start | bytes 2359296 | tf_op jit(solution)/shard_map/all_gather | solution.py:112
  91.0 80.9 %all-gather.17.cloned.1.call-start = ((), (), s32[]{:S(2)}) async-start(), calls=%async_computation.17 | async-start | bytes 1253376 | tf_op jit(solution)/shard_map/all_gather | solution.py:78
  91.6 91.0 %all-gather.15.cloned.1.call-start = ((), (), s32[]{:S(2)}) async-start(), calls=%async_computation.16 | async-start | bytes 2359296 | tf_op jit(solution)/shard_map/all_gather | solution.py:111
  98.4 113.9 %all-gather.13.cloned.1.call-start = ((), (), s32[]{:S(2)}) async-start(), calls=%async_computation.15 | async-start | bytes 2359296 | tf_op jit(solution)/shard_map/all_gather | solution.py:112
  231.2 41.3 %all-to-all-start = ((bf16[16,64,768]{2,1,0:T(8,128)(2,1)}), bf16[16,64,768]{2,1,0:T(8,128)(2,1)}, u32[]{:S(2)}, u32[]{:S(2)}) async-start(bf16[16,64,768]{2,1,0:T(8,128)(2,1)} %bitcast.435), calls=%async_computation | async-start | bytes 3145728 | tf_op jit(solution)/shard_map/all_to_all | solution.py:152
  272.5 42.0 %all-to-all-start.1 = ((bf16[16,64,768]{2,1,0:T(8,128)(2,1)}), bf16[16,64,768]{2,1,0:T(8,128)(2,1)}, u32[]{:S(2)}, u32[]{:S(2)}) async-start(bf16[16,64,768]{2,1,0:T(8,128)(2,1)} %bitcast.438), calls=%async_computation.1 | async-start | bytes 3145728 | tf_op jit(solution)/shard_map/all_to_all | solution.py:152
  304.5 39.3 %collective-permute-start.1 = (bf16[1,64,768]{2,1,0:T(8,128)(2,1)}, bf16[1,64,768]{2,1,0:T(8,128)(2,1)}, u32[]{:S(2)}, u32[]{:S(2)}) collective-permute-start(bf16[1,64,768]{2,1,0:T(8,128)(2,1)} %get-tuple-element.86), channel_id=1, source_target_pairs={{0,2},{1,3},{2,0},{3,1},{4,6},{5,7},{6,4},{7,5},{8,10},{9,11},{10,... | collective-permute-start | bytes 294920 | tf_op jit(solution)/shard_map/ppermute | solution.py:165
  305.9 39.4 %collective-permute-start.2 = (bf16[1,64,768]{2,1,0:T(8,128)(2,1)}, bf16[1,64,768]{2,1,0:T(8,128)(2,1)}, u32[]{:S(2)}, u32[]{:S(2)}) collective-permute-start(bf16[1,64,768]{2,1,0:T(8,128)(2,1)} %get-tuple-element.85), channel_id=1, source_target_pairs={{0,3},{1,2},{2,1},{3,0},{4,7},{5,6},{6,5},{7,4},{8,11},{9,10},{10,... | collective-permute-start | bytes 294920 | tf_op jit(solution)/shard_map/ppermute | solution.py:165
  306.1 44.1 %collective-permute-start.3 = (bf16[1,64,768]{2,1,0:T(8,128)(2,1)}, bf16[1,64,768]{2,1,0:T(8,128)(2,1)}, u32[]{:S(2)}, u32[]{:S(2)}) collective-permute-start(bf16[1,64,768]{2,1,0:T(8,128)(2,1)} %get-tuple-element.84), channel_id=1, source_target_pairs={{0,4},{1,5},{2,6},{3,7},{4,0},{5,1},{6,2},{7,3},{8,12},{9,13},{10,... | collective-permute-start | bytes 294920 | tf_op jit(solution)/shard_map/ppermute | solution.py:165
  307.9 44.2 %collective-permute-start.4 = (bf16[1,64,768]{2,1,0:T(8,128)(2,1)}, bf16[1,64,768]{2,1,0:T(8,128)(2,1)}, u32[]{:S(2)}, u32[]{:S(2)}) collective-permute-start(bf16[1,64,768]{2,1,0:T(8,128)(2,1)} %get-tuple-element.83), channel_id=1, source_target_pairs={{0,5},{1,4},{2,7},{3,6},{4,1},{5,0},{6,3},{7,2},{8,13},{9,12},{10,... | collective-permute-start | bytes 294920 | tf_op jit(solution)/shard_map/ppermute | solution.py:165
  433.8 41.3 %all-to-all-start.4 = ((bf16[16,64,768]{2,1,0:T(8,128)(2,1)}), bf16[16,64,768]{2,1,0:T(8,128)(2,1)}, u32[]{:S(2)}, u32[]{:S(2)}) async-start(bf16[16,64,768]{2,1,0:T(8,128)(2,1)} %bitcast.441), calls=%async_computation.6 | async-start | bytes 3145728 | tf_op jit(solution)/shard_map/all_to_all | solution.py:182
  475.1 41.1 %all-to-all-start.2 = ((bf16[16,64,768]{2,1,0:T(8,128)(2,1)}), bf16[16,64,768]{2,1,0:T(8,128)(2,1)S(1)}, u32[]{:S(2)}, u32[]{:S(2)}) async-start(bf16[16,64,768]{2,1,0:T(8,128)(2,1)} %bitcast.442), calls=%async_computation.2 | async-start | bytes 3145728 | tf_op jit(solution)/shard_map/all_to_all | solution.py:182
  516.2 41.4 %all-to-all-start.5 = ((bf16[16,64,768]{2,1,0:T(8,128)(2,1)}), bf16[16,64,768]{2,1,0:T(8,128)(2,1)}, u32[]{:S(2)}, u32[]{:S(2)}) async-start(bf16[16,64,768]{2,1,0:T(8,128)(2,1)} %bitcast.443), calls=%async_computation.7 | async-start | bytes 3145728 | tf_op jit(solution)/shard_map/all_to_all | solution.py:198
  557.6 40.9 %all-to-all-start.3 = ((bf16[16,64,768]{2,1,0:T(8,128)(2,1)}), bf16[16,64,768]{2,1,0:T(8,128)(2,1)}, u32[]{:S(2)}, u32[]{:S(2)}) async-start(bf16[16,64,768]{2,1,0:T(8,128)(2,1)} %bitcast.103), calls=%async_computation.3 | async-start | bytes 3145728 | tf_op jit(solution)/shard_map/all_to_all | solution.py:198
  565.0 226.9 %reduce-scatter.10.cloned.1.call-start = ((), (), s32[]{:S(2)}) async-start(), calls=%async_computation.20 | async-start | bytes 2359296 | tf_op jit(solution)/shard_map/reduce_scatter | solution.py:240
  653.0 138.9 %reduce-scatter.12.cloned.1.call-start = ((), (), s32[]{:S(2)}) async-start(), calls=%async_computation.21 | async-start | bytes 2359296 | tf_op jit(solution)/shard_map/reduce_scatter | solution.py:246
  671.3 127.5 %reduce-scatter.14.cloned.1.call-start = ((), (), s32[]{:S(2)}) async-start(), calls=%async_computation.22 | async-start | bytes 2359296 | tf_op jit(solution)/shard_map/reduce_scatter | solution.py:240
  712.0 86.7 %reduce-scatter.16.cloned.1.call-start = ((), (), s32[]{:S(2)}) async-start(), calls=%async_computation.23 | async-start | bytes 2359296 | tf_op jit(solution)/shard_map/reduce_scatter | solution.py:246
  726.6 146.5 %reduce-scatter.24.cloned.1.call-start = ((), (), s32[]{:S(2)}) async-start(), calls=%async_computation.27 | async-start | bytes 7077888 | tf_op jit(solution)/shard_map/reduce_scatter | solution.py:272
  747.3 136.3 %reduce-scatter.22.cloned.1.call-start = ((), (), s32[]{:S(2)}) async-start(), calls=%async_computation.26 | async-start | bytes 7077888 | tf_op jit(solution)/shard_map/reduce_scatter | solution.py:269
  764.7 123.5 %reduce-scatter.20.cloned.1.call-start = ((), (), s32[]{:S(2)}) async-start(), calls=%async_computation.25 | async-start | bytes 2433024 | tf_op jit(solution)/shard_map/reduce_scatter | solution.py:264
  770.0 241.5 %reduce-scatter.18.cloned.1.call-start = ((), (), s32[]{:S(2)}) async-start(), calls=%async_computation.24 | async-start | bytes 7299072 | tf_op jit(solution)/shard_map/reduce_scatter | solution.py:263
  (132 other events, 2914.4 us)
Sparse Core Ops, SparseCore 0:
  10.8 73.9 all-gather.10
  90.4 8.3 all-gather.20
  100.9 10.9 all-gather.18
  114.6 57.2 all-gather.16
  173.9 8.6 all-gather.14
  184.5 10.9 all-gather.12
  653.1 10.7 reduce-scatter.9
  671.4 10.6 reduce-scatter.11
  712.2 10.9 reduce-scatter.13
  726.7 11.1 reduce-scatter.15
  747.4 14.5 reduce-scatter.23
  764.9 15.0 reduce-scatter.21
  785.8 100.3 reduce-scatter.19
  893.2 118.1 reduce-scatter.17
